TPU v7x, 32 devices: a whole 2x2x4 slice. The times are simulated.
32 devices in a mesh: groups: 2 (over y), blk: 4 (over z), occ: 2 (over x), rep: 2 (over core).
Axes of the slice: x: 2, y: 2, z: 4, core: 2. Of those that a mesh axis runs over, the one named last changes fastest.
Arguments:
- amplitudes: float32 [1536, 4, 256], P(('groups', 'occ'), 'blk', 'rep'), parts along dimension 0, may hold values from -6 to 6
- integrals: float32 [4096, 4, 256], P(('groups', 'blk'), None, 'rep'), parts along dimension 0, may hold values from -0.0625 to 0.0625, as said below
Outputs:
- symmetrized: float32 [1536, 2048], P(('groups', 'occ'), ('blk', 'rep')), parts along dimension 0
There are 2 independent parts, one for each index of `groups`. A program takes and returns all parts, laid end to end along the dimension named above; each array names one. Nothing has to cross between parts.
Inputs may be any that keep to these rules, and one draw needn't show every extreme that they name: integrals[2047 - a, 3 - c, 255 - w] equals integrals[a, c, w]: pairs are listed so that a pair's transpose stands at the mirrored position.
All inputs are finite; a program needn't handle non-finite values.
Results may differ from a plain program's by a relative error of at most 0.00007.
Values sent between devices are 32-bit elements; how exact they have to be, the bound alone decides.
No kernel may reach another device: no remote copies, remote signals or barrier semaphores. Data moves between devices by JAX's collectives and lax.ppermute only.
A program may use at most 64 MiB of HBM per device.

v0:
```python
import jax
import jax.numpy as jnp
from jax import lax
from jax.sharding import PartitionSpec as P


def swapped(array, axis, stride):
    return lax.ppermute(array, axis, [(i, i ^ 1 << stride) for i in range(lax.axis_size(axis))])


def contract(running, portion, integrals):
    left_rows = portion.reshape(portion.shape[0], -1)
    right_rows = integrals.reshape(integrals.shape[0], -1)
    return running + lax.dot_general(
        left_rows,
        right_rows,
        (((1,), (1,)), ((), ())),
        precision=lax.Precision.HIGHEST,
        preferred_element_type=jnp.float32,
    )


def shards(amplitudes, integrals):
    zeros_init = jnp.zeros((amplitudes.shape[0], integrals.shape[0]), jnp.float32)
    partner = amplitudes
    for position in range(lax.axis_size(("occ", "rep")).bit_length() - 1):
        partner = swapped(partner, ("occ", "rep"), position)
    reflected_rows = partner[::-1, :, ::-1]
    running = zeros_init
    direct = lax.all_gather(amplitudes, "blk", axis=1, tiled=True)
    reflected = lax.all_gather(reflected_rows, "blk", axis=1, tiled=True)
    running = contract(running, direct, integrals)
    partial_sum = contract(running, reflected[:, ::-1, :], integrals)
    ladder = lax.psum_scatter(partial_sum, "rep", scatter_dimension=1, tiled=True)
    return ladder


def solution(mesh):
    return jax.shard_map(
        shards,
        mesh=mesh,
        in_specs=(P(("groups", "occ"), "blk", "rep"), P(("groups", "blk"), None, "rep")),
        out_specs=P(("groups", "occ"), ("blk", "rep")),
        check_vma=False,
    )
```

profile of v0, /device:TPU:0, one launch (start us, length us, event | category | flops | bytes accessed | tf_op | source)
XLA Modules:
  0.0 67.1 jit_solution(17421300760304804914)
XLA Ops:
  6.5 0.0 copy-start
  6.5 0.0 reduce-scatter.2.cloned.1.call-start
  6.5 0.5 collective-permute-start
  7.0 1.3 %collective-permute-done = f32[384,1,128]{2,0,1:T(8,128)S(1)} collective-permute-done((f32[384,1,128]{2,0,1:T(8,128)}, f32[384,1,128]{2,0,1:T(8,128)S(1)}, u32[]{:S(2)}, u32[]{:S(2)}) %collective-permute-start) | collective-permute-done | bytes 196640 | tf_op jit(solution)/shard_map/ppermute | solution.py:8
  8.3 2.8 %collective-permute-start.1 = (f32[384,1,128]{2,0,1:T(8,128)S(1)}, f32[384,1,128]{2,0,1:T(8,128)S(1)}, u32[]{:S(2)}, u32[]{:S(2)}) collective-permute-start(f32[384,1,128]{2,0,1:T(8,128)S(1)} %collective-permute-done), channel_id=1, source_target_pairs={{0,2},{1,3},{2,0},{3,1},{4,6},{5,7},{6,4},{7,5},{8,10},{9,11},{10,... | collective-permute-start | bytes 589832 | tf_op jit(solution)/shard_map/ppermute | solution.py:8
  11.2 20.0 %all_gather.6 = f32[384,4,128]{2,0,1:T(8,128)S(1)} all-gather(f32[384,1,128]{2,0,1:T(8,128)} %bitcast.11), channel_id=1, replica_groups=mesh['groups'=2,'blk'=4,'occ'=2,'rep'=2] {'blk'}, dimensions={1}, use_global_device_ids=true | all-gather | bytes 983040 | tf_op jit(solution)/shard_map/all_gather | solution.py:30
  31.2 0.0 copy-done
  31.2 1.5 %convolution_bitcast_fusion.1 = f32[384,512]{1,0:T(8,128)S(1)} fusion(f32[384,4,128]{2,0,1:T(8,128)S(1)} %all_gather.6, f32[512,4,128]{2,1,0:T(4,128)S(1)} %copy-done), kind=kOutput, calls=%fused_computation.1 | convolution fusion | flops 1207959552 | bytes 2621440 | tf_op jit(solution)/shard_map/dot_general | solution.py:14
  32.7 0.0 collective-permute-done.1
  32.7 0.3 rev.6
  32.9 17.7 %all_gather.7 = f32[384,4,128]{2,0,1:T(8,128)S(1)} all-gather(f32[384,1,128]{2,0,1:T(8,128)S(1)} %rev.6), channel_id=1, replica_groups=mesh['groups'=2,'blk'=4,'occ'=2,'rep'=2] {'blk'}, dimensions={1}, use_global_device_ids=true | all-gather | bytes 983040 | tf_op jit(solution)/shard_map/all_gather | solution.py:31
  50.7 0.1 rev.7
  50.7 2.3 %fusion = f32[384,512]{1,0:T(8,128)} fusion(f32[384,512]{1,0:T(8,128)S(1)} %convolution_bitcast_fusion.1, f32[384,4,128]{2,0,1:T(8,128)S(1)} %rev.7, f32[512,4,128]{2,1,0:T(4,128)S(1)} %copy-done), kind=kOutput, calls=%fused_computation.2 | convolution fusion | flops 1208156160 | bytes 3407872 | tf_op jit(solution)/shard_map/dot_general | solution.py:14
  53.1 0.0 reduce-scatter.2.cloned.1.call-update
  53.1 7.1 %reduce-scatter.2.cloned.1.call-done = f32[384,256]{1,0:T(8,128)} async-done(((f32[384,512]{1,0:T(8,128)}), f32[384,256]{1,0:T(8,128)}) %reduce-scatter.2.cloned.1.call-update) | async-done | bytes 393232 | tf_op jit(solution)/shard_map/reduce_scatter | solution.py:34
Async XLA Ops:
  6.5 24.7 %copy-start = (f32[512,4,128]{2,1,0:T(4,128)S(1)}, f32[512,4,128]{2,1,0:T(4,128)}, u32[]{:S(2)}) copy-start(f32[512,4,128]{2,1,0:T(4,128)} %param.3) | copy-start | bytes 3145732
  6.5 53.7 %reduce-scatter.2.cloned.1.call-start = ((), (), s32[]{:S(2)}) async-start(), calls=%async_computation.1 | async-start | bytes 1179648 | tf_op jit(solution)/shard_map/reduce_scatter | solution.py:34
  6.5 1.8 %collective-permute-start = (f32[384,1,128]{2,0,1:T(8,128)}, f32[384,1,128]{2,0,1:T(8,128)S(1)}, u32[]{:S(2)}, u32[]{:S(2)}) collective-permute-start(f32[384,1,128]{2,0,1:T(8,128)} %bitcast.10), channel_id=1, source_target_pairs={{0,1},{1,0},{2,3},{3,2},{4,5},{5,4},{6,7},{7,6},{8,9},{9,8},{10,11... | collective-permute-start | bytes 589832 | tf_op jit(solution)/shard_map/ppermute | solution.py:8
  8.3 24.3 %collective-permute-start.1 = (f32[384,1,128]{2,0,1:T(8,128)S(1)}, f32[384,1,128]{2,0,1:T(8,128)S(1)}, u32[]{:S(2)}, u32[]{:S(2)}) collective-permute-start(f32[384,1,128]{2,0,1:T(8,128)S(1)} %collective-permute-done), channel_id=1, source_target_pairs={{0,2},{1,3},{2,0},{3,1},{4,6},{5,7},{6,4},{7,5},{8,10},{9,11},{10,... | collective-permute-start | bytes 589832 | tf_op jit(solution)/shard_map/ppermute | solution.py:8
Sparse Core Ops, SparseCore 0:
  53.2 6.9 reduce-scatter.1
where the time goes:
time: 67.2 us; the launch traced here: 67.1 us
  blocking collectives  37.8 us (56%)
  between operations  13.4 us (20%)
  waiting for transfers between devices  8.44 us (13%)
  matrix products  3.8 us (6%)
  starting transfers between devices  3.34 us (5%)
    all_gather x1, blocking collectives, shards(): direct = lax.all_gather(amplitudes, 'blk', axis=1, tiled=True)  20 us
    all_gather x1, blocking collectives, shards(): reflected = lax.all_gather(reflected_rows, 'blk', axis=1, tiled=True)  17.7 us
    reduce_scatter x1, waiting for transfers between devices, shards(): lax.psum_scatter(partial_sum, 'rep', scatter_dimension=1, tiled=True)  7.14 us
    dot_general x2, matrix products, contract(): lax.dot_general(left_rows, right_rows, (((1,), (1,)), ((), ())), precisio...  3.8 us
    ppermute x2, starting transfers between devices, swapped(): lax.ppermute(array, axis, [(i, i ^ 1 << stride) for i in range(lax.axis_s...  3.34 us
  transfers between devices with their start and end apart: 3, of which 2 were waited for; matrix products, arithmetic and copies ran while one was open for 2% of the time, Pallas kernels for 0%

commit v1 on v0

v1 whole, which is shorter than its diff:
```python
import jax
import jax.numpy as jnp
from jax import lax
from jax.sharding import PartitionSpec as P

PLANE = ("blk", "occ", "rep")


def mirrored(array):
    size = lax.axis_size(PLANE)
    return lax.ppermute(array, PLANE, [(i, size - 1 - i) for i in range(size)])


def shifted(array, offset, flip):
    blks, occs, reps = (lax.axis_size(name) for name in PLANE)
    half = blks // 2
    pairs = []
    for blk in range(blks):
        target_blk = blk // half * half + (blk % half + offset) % half
        for occ in range(occs):
            for rep in range(reps):
                target = (target_blk, occs - 1 - occ, reps - 1 - rep) if flip else (target_blk, occ, rep)
                source_index = (blk * occs + occ) * reps + rep
                target_index = (target[0] * occs + target[1]) * reps + target[2]
                pairs.append((source_index, target_index))
    return lax.ppermute(array, PLANE, pairs)


def product(rows, columns):
    return lax.dot_general(
        rows,
        columns,
        (((1,), (1,)), ((), ())),
        precision=lax.Precision.HIGHEST,
        preferred_element_type=jnp.float32,
    )


def shards(amplitudes, integrals):
    blks, _, reps = (lax.axis_size(name) for name in PLANE)
    half = blks // 2
    blk = lax.axis_index("blk")
    rep = lax.axis_index("rep")
    width = integrals.shape[0] // reps
    depth = integrals.shape[2]

    own = amplitudes[:, 0, :]
    transposed = mirrored(own)
    summed = own + transposed[::-1, ::-1]
    summed_back = own[::-1, ::-1] + transposed

    def columns_of(position, owner):
        return lax.dynamic_slice(integrals, (owner * width, position, 0), (width, 1, depth))[:, 0, :]

    terms = []
    for offset in range(half):
        position = blk // half * half + (blk % half - offset) % half
        near = summed if offset == 0 else shifted(summed, offset, False)
        terms.append((near, position))
        terms.append((shifted(summed_back, offset, True), blks - 1 - position))
    others = sum(product(rows, columns_of(position, 1 - rep)) for rows, position in terms)
    mine = sum(product(rows, columns_of(position, rep)) for rows, position in terms)
    return mine + lax.ppermute(others, "rep", [(0, 1), (1, 0)])


def solution(mesh):
    return jax.shard_map(
        shards,
        mesh=mesh,
        in_specs=(P(("groups", "occ"), "blk", "rep"), P(("groups", "blk"), None, "rep")),
        out_specs=P(("groups", "occ"), ("blk", "rep")),
        check_vma=False,
    )
```

time: 67.2 us -> 32.4 us (0.48)
  blocking collectives: 37.8 us -> 0 us
  between operations: 13.4 us -> 0.11 us
  starting transfers between devices: 3.34 us -> 12 us
  waiting for transfers between devices: 8.44 us -> 12.3 us
  local copies, waits for them, and re-layouts: 0.33 us -> 3.21 us
  matrix products: 3.8 us -> 4.6 us
    all_gather x2 -> x0, blocking collectives: 37.8 us -> none  [the longest x1 20 us: shards(): direct = lax.all_gather(amplitudes, 'blk', axis=1, tiled=True)]
    ppermute x2 -> x5, waiting for transfers between devices: 1.28 us -> 12.3 us  [the longest x3 8.25 us: shifted(): return lax.ppermute(array, PLANE, pairs)]
    ppermute x2 -> x5, starting transfers between devices: 3.34 us -> 12 us  [the longest x3 6.46 us: shifted(): return lax.ppermute(array, PLANE, pairs)]
    reduce_scatter x1 -> x0, waiting for transfers between devices: 7.14 us -> none  [shards(): lax.psum_scatter(partial_sum, 'rep', scatter_dimension=1, tiled=True)]
    rev x2, local copies, waits for them, and re-layouts: 0.33 us -> 2.12 us  [the longest x1 1.87 us: shards(): summed_back = own[::-1, ::-1] + transposed]
    dynamic_slice x0 -> x1, local copies, waits for them, and re-layouts: none -> 1.08 us  [columns_of(): lax.dynamic_slice(integrals, (owner * width, position, 0), (width, 1, dep...]
    dot_general x2 -> x8, matrix products: 3.8 us -> 4.6 us  [product(): lax.dot_general(rows, columns, (((1,), (1,)), ((), ())), precision=lax.Pr...]
  transfers between devices with their start and end apart: 3 -> 5, of which waited for: 2 -> 3; matrix products, arithmetic and copies ran while one was open for 2% -> 17% of each run, Pallas kernels for 0% -> 0%
where the time goes in v1:
time: 32.4 us; the launch traced here: 32.2 us
  waiting for transfers between devices  12.3 us (38%)
  starting transfers between devices  12 us (37%)
  matrix products  4.6 us (14%)
  local copies, waits for them, and re-layouts  3.21 us (10%)
    ppermute x3, waiting for transfers between devices, shifted(): return lax.ppermute(array, PLANE, pairs)  8.25 us
    ppermute x3, starting transfers between devices, shifted(): return lax.ppermute(array, PLANE, pairs)  6.46 us
    ppermute x1, starting transfers between devices, mirrored(): return lax.ppermute(array, PLANE, [(i, size - 1 - i) for i in range(size)])  5.44 us
    dot_general x8, matrix products, product(): lax.dot_general(rows, columns, (((1,), (1,)), ((), ())), precision=lax.Pr...  4.6 us
    ppermute x1, waiting for transfers between devices, mirrored(): return lax.ppermute(array, PLANE, [(i, size - 1 - i) for i in range(size)])  3.77 us
    rev x1, local copies, waits for them, and re-layouts, shards(): summed_back = own[::-1, ::-1] + transposed  1.87 us
    dynamic_slice x1, local copies, waits for them, and re-layouts, columns_of(): lax.dynamic_slice(integrals, (owner * width, position, 0), (width, 1, dep...  1.08 us
  transfers between devices with their start and end apart: 5, of which 3 were waited for; matrix products, arithmetic and copies ran while one was open for 17% of the time, Pallas kernels for 0%

profile of v1, /device:TPU:0, one launch (start us, length us, event | category | flops | bytes accessed | tf_op | source)
XLA Modules:
  0.0 32.2 jit_solution(17055308851639268979)
XLA Ops:
  0.0 5.4 %collective-permute-start = (f32[384,128]{1,0:T(8,128)}, f32[384,128]{1,0:T(8,128)S(1)}, u32[]{:S(2)}, u32[]{:S(2)}) collective-permute-start(f32[384,128]{1,0:T(8,128)} %bitcast.25), channel_id=1, source_target_pairs={{0,15},{1,14},{2,13},{3,12},{4,11},{5,10},{6,9},{7,8},{8,7},{9,6},... | collective-permute-start | bytes 589832 | tf_op jit(solution)/shard_map/ppermute | solution.py:11
  5.4 1.9 %rev.7 = f32[384,128]{1,0:T(8,128)S(1)} reverse(f32[384,128]{1,0:T(8,128)} %bitcast.26), dimensions={0,1} | reverse | bytes 393216 | tf_op jit(solution)/shard_map/rev | solution.py:50
  7.3 3.8 %collective-permute-done = f32[384,128]{1,0:T(8,128)S(1)} collective-permute-done((f32[384,128]{1,0:T(8,128)}, f32[384,128]{1,0:T(8,128)S(1)}, u32[]{:S(2)}, u32[]{:S(2)}) %collective-permute-start) | collective-permute-done | bytes 196640 | tf_op jit(solution)/shard_map/ppermute | solution.py:11
  11.1 1.8 %collective-permute-start.1 = (f32[384,128]{1,0:T(8,128)S(1)}, f32[384,128]{1,0:T(8,128)S(1)}, u32[]{:S(2)}, u32[]{:S(2)}) collective-permute-start(f32[384,128]{1,0:T(8,128)S(1)} %add.82), channel_id=1, source_target_pairs={{0,3},{1,2},{2,1},{3,0},{4,7},{5,6},{6,5},{7,4},{8,11},{9,10},{10,... | collective-permute-start | bytes 589832 | tf_op jit(solution)/shard_map/ppermute | solution.py:26
  12.9 0.0 copy-done
  12.9 1.1 %constant_dynamic-slice_fusion.7 = (f32[256,1,128]{2,1,0:T(1,128)S(1)}, f32[256,1,128]{2,1,0:T(1,128)S(1)}, f32[256,1,128]{2,1,0:T(1,128)S(1)}, f32[256,1,128]{2...) fusion(f32[512,4,128]{2,1,0:T(4,128)S(1)} %copy-done, ...), kind=kLoop, calls=%fused_computation.14 | loop fusion | bytes 2097176 | tf_op jit(solution)/shard_map/dynamic_slice | solution.py:53
  14.0 0.0 copy-start.1
  14.0 3.8 %collective-permute-start.3 = (f32[384,128]{1,0:T(8,128)S(1)}, f32[384,128]{1,0:T(8,128)S(1)}, u32[]{:S(2)}, u32[]{:S(2)}) collective-permute-start(f32[384,128]{1,0:T(8,128)S(1)} %add.82), channel_id=1, source_target_pairs={{0,7},{1,6},{2,5},{3,4},{4,3},{5,2},{6,1},{7,0},{8,15},{9,14},{10,... | collective-permute-start | bytes 589832 | tf_op jit(solution)/shard_map/ppermute | solution.py:26
  17.9 0.3 rev.6
  18.1 0.0 copy-done.1
  18.2 0.8 %collective-permute-start.2 = (f32[384,128]{1,0:T(8,128)S(1)}, f32[384,128]{1,0:T(8,128)S(1)}, u32[]{:S(2)}, u32[]{:S(2)}) collective-permute-start(f32[384,128]{1,0:T(8,128)S(1)} %add.76), channel_id=1, source_target_pairs={{0,4},{1,5},{2,6},{3,7},{4,0},{5,1},{6,2},{7,3},{8,12},{9,13},{10,... | collective-permute-start | bytes 589832 | tf_op jit(solution)/shard_map/ppermute | solution.py:26
  19.0 0.0 collective-permute-done.1
  19.0 0.5 %fusion.8 = f32[384,256]{1,0:T(8,128)S(1)} fusion(f32[384,128]{1,0:T(8,128)S(1)} %collective-permute-done.1, f32[256,128]{1,0:T(8,128)S(1)} %bitcast.34), kind=kOutput, calls=%fused_computation.18 | convolution fusion | flops 150994944 | bytes 720896 | tf_op jit(solution)/shard_map/dot_general | solution.py:30
  19.5 8.2 %collective-permute-done.2 = f32[384,128]{1,0:T(8,128)S(1)} collective-permute-done((f32[384,128]{1,0:T(8,128)S(1)}, f32[384,128]{1,0:T(8,128)S(1)}, u32[]{:S(2)}, u32[]{:S(2)}) %collective-permute-start.2) | collective-permute-done | bytes 196640 | tf_op jit(solution)/shard_map/ppermute | solution.py:26
  27.7 0.5 %fusion.9 = f32[384,256]{1,0:T(8,128)S(1)} fusion(f32[384,128]{1,0:T(8,128)S(1)} %collective-permute-done.2, f32[256,128]{1,0:T(8,128)S(1)} %bitcast.33), kind=kOutput, calls=%fused_computation.19 | convolution fusion | flops 150994944 | bytes 720896 | tf_op jit(solution)/shard_map/dot_general | solution.py:30
  28.2 0.0 collective-permute-done.3
  28.2 0.5 %fusion.10 = f32[384,256]{1,0:T(8,128)S(1)} fusion(f32[384,128]{1,0:T(8,128)S(1)} %collective-permute-done.3, f32[256,128]{1,0:T(8,128)S(1)} %bitcast.32), kind=kOutput, calls=%fused_computation.20 | convolution fusion | flops 150994944 | bytes 720896 | tf_op jit(solution)/shard_map/dot_general | solution.py:30
  28.7 0.5 %fusion.2 = f32[384,256]{1,0:T(8,128)S(1)} fusion(f32[384,256]{1,0:T(8,128)S(1)} %fusion.10, f32[384,256]{1,0:T(8,128)S(1)} %fusion.9, f32[384,256]{1,0:T(8,128)S(1)} %fusion.8, f32[384,128]{1,0:T(8,128)S(1)} %add.76, f32[256,128]{1,0:T(8,128)S(1)} %bitcast.35), kind=kOutput, calls=%fused_computation.4 | convolution fusion | flops 151289856 | bytes 1900544 | tf_op jit(solution)/shard_map/dot_general | solution.py:30
  29.2 0.1 collective-permute-start.4
  29.3 0.5 %fusion.5 = f32[384,256]{1,0:T(8,128)S(1)} fusion(f32[384,128]{1,0:T(8,128)S(1)} %collective-permute-done.1, f32[256,128]{1,0:T(8,128)S(1)} %bitcast.31), kind=kOutput, calls=%fused_computation.15 | convolution fusion | flops 150994944 | bytes 720896 | tf_op jit(solution)/shard_map/dot_general | solution.py:30
  29.7 0.5 %fusion.6 = f32[384,256]{1,0:T(8,128)S(1)} fusion(f32[384,128]{1,0:T(8,128)S(1)} %collective-permute-done.2, f32[256,128]{1,0:T(8,128)S(1)} %bitcast.30), kind=kOutput, calls=%fused_computation.16 | convolution fusion | flops 150994944 | bytes 720896 | tf_op jit(solution)/shard_map/dot_general | solution.py:30
  30.2 0.5 %fusion.7 = f32[384,256]{1,0:T(8,128)S(1)} fusion(f32[384,128]{1,0:T(8,128)S(1)} %collective-permute-done.3, f32[256,128]{1,0:T(8,128)S(1)} %bitcast.29), kind=kOutput, calls=%fused_computation.17 | convolution fusion | flops 150994944 | bytes 720896 | tf_op jit(solution)/shard_map/dot_general | solution.py:30
  30.7 0.3 collective-permute-done.4
  31.0 1.3 %fusion.4 = f32[384,256]{1,0:T(8,128)} fusion(f32[384,256]{1,0:T(8,128)S(1)} %collective-permute-done.4, f32[384,256]{1,0:T(8,128)S(1)} %fusion.7, f32[384,256]{1,0:T(8,128)S(1)} %fusion.6, f32[384,256]{1,0:T(8,128)S(1)} %fusion.5, f32[384,128]{1,0:T(8,128)S(1)} %add.76, f32[256,128]{1,0:T(8,128)S(1)} %bitcast.28), kind=kOutput, calls=%fused_computation.6 | convolution fusion | flops 151388160 | bytes 2293760 | tf_op jit(solution)/shard_map/dot_general | solution.py:30
  (3 shorter events, 0.0 us)
Async XLA Ops:
  0.0 12.9 %copy-start = (f32[512,4,128]{2,1,0:T(4,128)S(1)}, f32[512,4,128]{2,1,0:T(4,128)}, u32[]{:S(2)}) copy-start(f32[512,4,128]{2,1,0:T(4,128)} %param.3) | copy-start | bytes 3145732
  0.0 11.1 %collective-permute-start = (f32[384,128]{1,0:T(8,128)}, f32[384,128]{1,0:T(8,128)S(1)}, u32[]{:S(2)}, u32[]{:S(2)}) collective-permute-start(f32[384,128]{1,0:T(8,128)} %bitcast.25), channel_id=1, source_target_pairs={{0,15},{1,14},{2,13},{3,12},{4,11},{5,10},{6,9},{7,8},{8,7},{9,6},... | collective-permute-start | bytes 589832 | tf_op jit(solution)/shard_map/ppermute | solution.py:11
  11.1 7.9 %collective-permute-start.1 = (f32[384,128]{1,0:T(8,128)S(1)}, f32[384,128]{1,0:T(8,128)S(1)}, u32[]{:S(2)}, u32[]{:S(2)}) collective-permute-start(f32[384,128]{1,0:T(8,128)S(1)} %add.82), channel_id=1, source_target_pairs={{0,3},{1,2},{2,1},{3,0},{4,7},{5,6},{6,5},{7,4},{8,11},{9,10},{10,... | collective-permute-start | bytes 589832 | tf_op jit(solution)/shard_map/ppermute | solution.py:26
  14.0 4.1 %copy-start.1 = (f32[384,1,128]{2,1,0:T(1,128)S(1)}, f32[384,1,128]{2,1,0:T(1,128)}, u32[]{:S(2)}) copy-start(f32[384,1,128]{2,1,0:T(1,128)} %param.2) | copy-start | bytes 589828
  14.0 14.2 %collective-permute-start.3 = (f32[384,128]{1,0:T(8,128)S(1)}, f32[384,128]{1,0:T(8,128)S(1)}, u32[]{:S(2)}, u32[]{:S(2)}) collective-permute-start(f32[384,128]{1,0:T(8,128)S(1)} %add.82), channel_id=1, source_target_pairs={{0,7},{1,6},{2,5},{3,4},{4,3},{5,2},{6,1},{7,0},{8,15},{9,14},{10,... | collective-permute-start | bytes 589832 | tf_op jit(solution)/shard_map/ppermute | solution.py:26
  18.2 9.5 %collective-permute-start.2 = (f32[384,128]{1,0:T(8,128)S(1)}, f32[384,128]{1,0:T(8,128)S(1)}, u32[]{:S(2)}, u32[]{:S(2)}) collective-permute-start(f32[384,128]{1,0:T(8,128)S(1)} %add.76), channel_id=1, source_target_pairs={{0,4},{1,5},{2,6},{3,7},{4,0},{5,1},{6,2},{7,3},{8,12},{9,13},{10,... | collective-permute-start | bytes 589832 | tf_op jit(solution)/shard_map/ppermute | solution.py:26
  29.2 1.8 %collective-permute-start.4 = (f32[384,256]{1,0:T(8,128)S(1)}, f32[384,256]{1,0:T(8,128)S(1)}, u32[]{:S(2)}, u32[]{:S(2)}) collective-permute-start(f32[384,256]{1,0:T(8,128)S(1)} %fusion.2), channel_id=1, source_target_pairs={{0,1},{1,0},{2,3},{3,2},{4,5},{5,4},{6,7},{7,6},{8,9},{9,8},{10,11... | collective-permute-start | bytes 1179656 | tf_op jit(solution)/shard_map/ppermute | solution.py:63
